TPU v7x, 128 devices: a whole 4x4x4 slice. The times are simulated.
128 devices in a mesh: dp: 16 (over z, y_hi, core), tensor: 8 (over x, y_lo).
Axes of the slice: x: 4, y: 4 (y_hi: 2, y_lo: 2; y = y_hi * 2 + y_lo), z: 4, core: 2. Of those that a mesh axis runs over, the one named last changes fastest.
Arguments:
- history: bfloat16 [4, 3072, 4096], P(None, 'dp'), may hold values from -6 to 6
- depth_weights: float32 [4], replicated, may hold values from 0.2 to 1
- depth_index: int32 [4], replicated, may hold values from 0 to 3
- gain: float32 [4096], replicated, may hold values from 0.1 to 1.9
- gate_blocks: bfloat16 [896, 128, 128], P(('tensor', 'dp')), may hold values from -0.1875 to 0.1875
- up_blocks: bfloat16 [896, 128, 128], P(('tensor', 'dp')), may hold values from -0.1875 to 0.1875
- down_blocks: bfloat16 [896, 128, 128], P(('tensor', 'dp')), may hold values from -0.09375 to 0.09375
- block_ids: int32 [896, 2], P('tensor'), may hold values from 0 to 31, as said below
- grad_out: bfloat16 [3072, 4096], P('dp'), may hold values from -16 to 16
Outputs:
- layer_out: bfloat16 [3072, 4096], P('dp', 'tensor')
- grad_mixed: float32 [3072, 4096], P('dp', 'tensor')
- grad_gate: float32 [896, 128, 128], P(('tensor', 'dp'))
- grad_up: float32 [896, 128, 128], P(('tensor', 'dp'))
- grad_down: float32 [896, 128, 128], P(('tensor', 'dp'))
- grad_depth: float32 [4], replicated
- grad_gain: float32 [4096], P('tensor')
Inputs may be any that keep to these rules, and one draw needn't show every extreme that they name: `block_ids`: within the 112 rows of one index of tensor the pairs are distinct; column 0 is a row block below 32, column 1 a column block below 14 counted within that index's hidden units.
All inputs are finite; a program needn't handle non-finite values.
Results may differ from a plain program's by a relative error of at most 0.025.
Values may be sent and summed in bfloat16 or wider, within the bound.
No kernel may reach another device: no remote copies, remote signals or barrier semaphores. Data moves between devices by JAX's collectives and lax.ppermute only.
A program may use at most 192 MiB of HBM per device.

v0:
```python
import jax
import jax.numpy as jnp
from jax import lax
from jax.sharding import PartitionSpec as P

FF = 14336
EPSILON = 1e-05


def norm_rows(mixed, gain):
    scale_inv = lax.rsqrt(jnp.mean(mixed * mixed, axis=-1, keepdims=True) + EPSILON)
    return mixed * scale_inv * gain


def per_device(
    history,
    depth_weights,
    depth_index,
    gain,
    gate_blocks,
    up_blocks,
    down_blocks,
    block_ids,
    grad_out,
):
    tok_rows = history.shape[1]
    width = history.shape[2]
    block_size = gate_blocks.shape[1]
    row_blocks = width // block_size
    tensor_count = lax.axis_size("tensor")
    col_blocks = FF // block_size // tensor_count
    share_width = width // tensor_count
    share_start = lax.axis_index("tensor") * share_width
    mixed = jnp.zeros((tok_rows, width), jnp.float32)
    for layer_slot in range(depth_index.shape[0]):
        earlier = lax.dynamic_index_in_dim(history, depth_index[layer_slot], 0, keepdims=False)
        mixed = mixed + depth_weights[layer_slot] * earlier.astype(jnp.float32)
    scale_inv = lax.rsqrt(jnp.mean(mixed * mixed, axis=-1, keepdims=True) + EPSILON)
    normed = (mixed * scale_inv * gain).astype(jnp.bfloat16)
    normed3 = normed.reshape(tok_rows, row_blocks, block_size)
    out3 = grad_out.reshape(tok_rows, row_blocks, block_size)
    row_ids = block_ids[:, 0]
    col_ids = block_ids[:, 1]
    zero_cols = jnp.zeros((tok_rows, col_blocks, block_size), jnp.float32)
    zero_rows = jnp.zeros((tok_rows, row_blocks, block_size), jnp.float32)

    def select():
        return (row_ids, col_ids)

    gate_all, up_all, down_all = (
        lax.all_gather(gate_blocks, "dp", axis=0, tiled=True),
        lax.all_gather(up_blocks, "dp", axis=0, tiled=True),
        lax.all_gather(down_blocks, "dp", axis=0, tiled=True),
    )
    pieces = (gate_all, up_all)
    rows_here, cols_here = select()
    picked = jnp.take(normed3, rows_here, axis=1)
    gate_part = jnp.einsum("tbi,bij->tbj", picked, pieces[0], preferred_element_type=jnp.float32)
    up_part = jnp.einsum("tbi,bij->tbj", picked, pieces[1], preferred_element_type=jnp.float32)
    gate_pre = zero_cols.at[:, cols_here].add(gate_part)
    up_pre = zero_cols.at[:, cols_here].add(up_part)
    hidden = (jax.nn.silu(gate_pre) * up_pre).astype(jnp.bfloat16)
    rows_here, cols_here = select()
    picked = jnp.take(hidden, cols_here, axis=1)
    product = jnp.einsum("tbi,bij->tbj", picked, down_all, preferred_element_type=jnp.float32)
    ffn3 = zero_rows.at[:, rows_here].add(product)
    ffn_share = lax.psum_scatter(
        ffn3.reshape(tok_rows, width).astype(jnp.bfloat16),
        "tensor",
        scatter_dimension=1,
        tiled=True,
    ).astype(jnp.float32)
    mixed_share = lax.dynamic_slice_in_dim(mixed, share_start, share_width, 1)
    layer_out = (mixed_share + ffn_share).astype(jnp.bfloat16)
    rows_here, cols_here = select()
    picked = jnp.take(out3, rows_here, axis=1)
    product = jnp.einsum("tbj,bij->tbi", picked, down_all, preferred_element_type=jnp.float32)
    grad_hidden = zero_cols.at[:, cols_here].add(product)
    sigmoid_gate = jax.nn.sigmoid(gate_pre)
    grad_gate_pre = (
        grad_hidden * up_pre * sigmoid_gate * (1.0 + gate_pre * (1.0 - sigmoid_gate))
    ).astype(jnp.bfloat16)
    grad_up_pre = (grad_hidden * gate_pre * sigmoid_gate).astype(jnp.bfloat16)
    pieces = (gate_all, up_all)
    rows_here, cols_here = select()
    picked_gate = jnp.take(grad_gate_pre, cols_here, axis=1)
    picked_up = jnp.take(grad_up_pre, cols_here, axis=1)
    contrib = jnp.einsum("tbj,bij->tbi", picked_gate, pieces[0], preferred_element_type=jnp.float32)
    contrib = contrib + jnp.einsum(
        "tbj,bij->tbi", picked_up, pieces[1], preferred_element_type=jnp.float32
    )
    grad_normed3 = zero_rows.at[:, rows_here].add(contrib)
    rows_here, cols_here = select()
    picked_in = jnp.take(normed3, rows_here, axis=1)
    picked_out = jnp.take(out3, rows_here, axis=1)
    picked_gate = jnp.take(grad_gate_pre, cols_here, axis=1)
    picked_up = jnp.take(grad_up_pre, cols_here, axis=1)
    picked_hidden = jnp.take(hidden, cols_here, axis=1)
    gate_term = jnp.einsum(
        "tbi,tbj->bij", picked_in, picked_gate, preferred_element_type=jnp.float32
    )
    up_term = jnp.einsum("tbi,tbj->bij", picked_in, picked_up, preferred_element_type=jnp.float32)
    down_term = jnp.einsum(
        "tbi,tbj->bij", picked_hidden, picked_out, preferred_element_type=jnp.float32
    )
    block_grads = lax.psum_scatter(
        jnp.stack([gate_term, up_term, down_term], axis=1).astype(jnp.bfloat16),
        "dp",
        scatter_dimension=0,
        tiled=True,
    ).astype(jnp.float32)
    grad_normed = grad_normed3.reshape(tok_rows, width)
    full_grad = lax.psum(grad_normed.astype(jnp.bfloat16), "tensor").astype(jnp.float32)
    ignored, pull_back = jax.vjp(norm_rows, mixed, gain)
    grad_x, gain_rows = pull_back(full_grad)
    grad_full = grad_out.astype(jnp.float32) + grad_x
    grad_mixed = lax.dynamic_slice_in_dim(grad_full, share_start, share_width, 1)
    gain_part = lax.dynamic_slice_in_dim(gain_rows, share_start, share_width, 0)
    depth_list = []
    for layer_slot in range(depth_index.shape[0]):
        earlier = lax.dynamic_index_in_dim(history, depth_index[layer_slot], 0, keepdims=False)
        depth_list.append(jnp.sum(grad_full * earlier.astype(jnp.float32)))
    gain_sum, depth_sum = lax.psum((gain_part, jnp.stack(depth_list)), "dp")
    return (
        layer_out,
        grad_mixed,
        block_grads[:, 0],
        block_grads[:, 1],
        block_grads[:, 2],
        depth_sum,
        gain_sum,
    )


def solution(mesh):
    placed = (
        P(None, "dp", None),
        P(),
        P(),
        P(),
        P(("tensor", "dp"), None, None),
        P(("tensor", "dp"), None, None),
        P(("tensor", "dp"), None, None),
        P("tensor", None),
        P("dp", None),
    )
    return jax.shard_map(
        per_device,
        mesh=mesh,
        in_specs=placed,
        out_specs=(
            P("dp", "tensor"),
            P("dp", "tensor"),
            P(("tensor", "dp"), None, None),
            P(("tensor", "dp"), None, None),
            P(("tensor", "dp"), None, None),
            P(),
            P("tensor"),
        ),
        check_vma=False,
    )
```

profile of v0, /device:TPU:0, one launch (start us, length us, event | category | flops | bytes accessed | tf_op | source)
XLA Modules:
  0.0 650.3 jit_solution(3859835161289719291)
XLA Ops:
  20.0 7.3 %fusion.43 = f32[24,8,32,128]{3,1,2,0:T(8,128)S(1)} fusion(f32[]{:T(128)} %bitcast.9, f32[]{:T(128)} %bitcast.6, f32[]{:T(128)} %bitcast.3, f32[]{:T(128)} %bitcast, bf16[4,192,4096]{2,1,0:T(8,128)(2,1)} %param.13, s32[]{:T(128)S(6)} %select_n.49, s32[]{:T(128)S(6)} %select_n.48, s32[]{:T(128)S(6)} %select_n.47, s32[]{:T(128)S(6)} %select_n.46), kind=kLoop, calls=%fused_computation.71 | loop fusion | flops 8650752 | bytes 9437216
  28.1 5.6 multiply_reduce_fusion
  35.7 3.8 gather_fusion
  39.9 3.7 gather_fusion.2
  43.7 22.0 %all-gather.4.cloned.1.call-done = bf16[112,128,128]{2,1,0:T(8,128)(2,1)} async-done(((bf16[7,128,128]{2,1,0:T(8,128)(2,1)}), bf16[112,128,128]{2,1,0:T(8,128)(2,1)}) %all-gather.4.cloned.1.call-update) | async-done | bytes 3670032 | tf_op jit(solution)/shard_map/all_gather | solution.py:51
  65.7 9.4 %fusion.19 = f32[112,192,128]{2,1,0:T(8,128)} fusion(bf16[112,128,128]{2,1,0:T(8,128)(2,1)} %all-gather.4.cloned.1.call-done, bf16[112,192,128]{2,1,0:T(8,128)(2,1)} %gather_fusion, pred[112]{0:T(512)(128)(4,1)S(1)} %get-tuple-element.30), kind=kOutput, calls=%fused_computation.30 | convolution fusion | flops 707395584 | bytes 20185200 | tf_op jit(solution)/shard_map/tbi,bij->tbj/dot_general | solution.py:58
  75.2 18.7 %scatter_fusion = f32[192,14,128]{2,0,1:T(8,128)S(1)} fusion(f32[192,14,128]{2,0,1:T(8,128)S(1)} %broadcast_in_dim.37.clone, s32[112]{0:T(128)S(1)} %get-tuple-element.32, f32[112,192,128]{2,1,0:T(8,128)} %fusion.19), kind=kCustom, calls=%fused_computation.5 | custom fusion | flops 2752512 | bytes 33030592 | tf_op jit(solution)/shard_map/scatter-add | solution.py:60
  93.9 25.2 %all-gather.6.cloned.1.call-done = bf16[112,128,128]{2,1,0:T(8,128)(2,1)} async-done(((bf16[7,128,128]{2,1,0:T(8,128)(2,1)}), bf16[112,128,128]{2,1,0:T(8,128)(2,1)}) %all-gather.6.cloned.1.call-update) | async-done | bytes 3670032 | tf_op jit(solution)/shard_map/all_gather | solution.py:52
  119.1 9.4 %fusion.17 = f32[112,192,128]{2,1,0:T(8,128)} fusion(bf16[112,128,128]{2,1,0:T(8,128)(2,1)} %all-gather.6.cloned.1.call-done, bf16[112,192,128]{2,1,0:T(8,128)(2,1)} %gather_fusion, pred[112]{0:T(512)(128)(4,1)S(1)} %get-tuple-element.30), kind=kOutput, calls=%fused_computation.28 | convolution fusion | flops 707395584 | bytes 20185200 | tf_op jit(solution)/shard_map/tbi,bij->tbj/dot_general | solution.py:59
  128.7 18.3 %scatter_fusion.1 = f32[192,14,128]{2,0,1:T(8,128)S(1)} fusion(f32[192,14,128]{2,0,1:T(8,128)S(1)} %broadcast_in_dim.37.clone.2, s32[112]{0:T(128)S(1)} %get-tuple-element.32, f32[112,192,128]{2,1,0:T(8,128)} %fusion.17), kind=kCustom, calls=%fused_computation.6 | custom fusion | flops 2752512 | bytes 33030592 | tf_op jit(solution)/shard_map/scatter-add | solution.py:61
  147.0 25.6 %all-gather.8.cloned.1.call-done = bf16[112,128,128]{2,1,0:T(8,128)(2,1)} async-done(((bf16[7,128,128]{2,1,0:T(8,128)(2,1)}), bf16[112,128,128]{2,1,0:T(8,128)(2,1)}) %all-gather.8.cloned.1.call-update) | async-done | bytes 3670032 | tf_op jit(solution)/shard_map/all_gather | solution.py:53
  172.6 10.2 %fusion.10 = f32[112,192,128]{2,1,0:T(8,128)} fusion(bf16[112,128,128]{2,1,0:T(8,128)(2,1)} %all-gather.8.cloned.1.call-done, bf16[112,192,128]{2,1,0:T(8,128)(2,1)} %gather_fusion.2, pred[112]{0:T(512)(128)(4,1)S(1)} %get-tuple-element.30), kind=kOutput, calls=%fused_computation.21 | convolution fusion | flops 707395584 | bytes 20185200 | tf_op jit(solution)/shard_map/tbj,bij->tbi/dot_general | solution.py:77
  183.0 18.4 %scatter_fusion.3 = f32[192,14,128]{2,0,1:T(8,128)S(1)} fusion(f32[192,14,128]{2,0,1:T(8,128)S(1)} %broadcast_in_dim.37.clone.1, s32[112]{0:T(128)S(1)} %get-tuple-element.32, f32[112,192,128]{2,1,0:T(8,128)} %fusion.10), kind=kCustom, calls=%fused_computation.8 | custom fusion | flops 2752512 | bytes 33030592 | tf_op jit(solution)/shard_map/scatter-add | solution.py:78
  201.4 3.3 multiply_convert_fusion.1
  204.7 4.9 gather_fusion.4
  209.5 3.8 gather_fusion.3
  213.3 10.4 %fusion.2 = f32[112,192,128]{2,1,0:T(8,128)} fusion(bf16[112,128,128]{2,1,0:T(8,128)(2,1)} %all-gather.6.cloned.1.call-done, bf16[112,192,128]{2,1,0:T(8,128)(2,1)} %gather_fusion.4, pred[112]{0:T(512)(128)(4,1)S(1)} %get-tuple-element.18), kind=kOutput, calls=%fused_computation.13 | convolution fusion | flops 707395584 | bytes 20185200 | tf_op jit(solution)/shard_map/tbj,bij->tbi/dot_general | solution.py:89
  223.7 12.0 %fusion.29 = f32[112,192,128]{2,1,0:T(8,128)} fusion(f32[112,192,128]{2,1,0:T(8,128)} %fusion.2, bf16[112,128,128]{2,1,0:T(8,128)(2,1)} %all-gather.4.cloned.1.call-done, bf16[112,192,128]{2,1,0:T(8,128)(2,1)S(1)} %copy-done.3, pred[112]{0:T(512)(128)(4,1)S(1)} %get-tuple-element.18), kind=kOutput, calls=%fused_computation.56 | convolution fusion | flops 710148096 | bytes 31195248 | tf_op jit(solution)/shard_map/tbj,bij->tbi/dot_general | solution.py:88
  236.0 18.3 %scatter_fusion.4 = f32[192,32,128]{2,0,1:T(8,128)S(1)} fusion(f32[192,32,128]{2,0,1:T(8,128)S(1)} %broadcast_in_dim.36.clone.1, s32[112]{0:T(128)S(1)} %get-tuple-element.33, f32[112,192,128]{2,1,0:T(8,128)} %fusion.29), kind=kCustom, calls=%fused_computation.9 | custom fusion | flops 2752512 | bytes 33030592 | tf_op jit(solution)/shard_map/scatter-add | solution.py:92
  256.8 3.8 gather_fusion.1
  260.6 9.6 %fusion.13 = f32[112,192,128]{2,1,0:T(8,128)} fusion(bf16[112,128,128]{2,1,0:T(8,128)(2,1)} %all-gather.8.cloned.1.call-done, bf16[112,192,128]{2,1,0:T(8,128)(2,1)} %gather_fusion.1, pred[112]{0:T(512)(128)(4,1)S(1)} %get-tuple-element.18), kind=kOutput, calls=%fused_computation.24 | convolution fusion | flops 707395584 | bytes 20185200 | tf_op jit(solution)/shard_map/tbi,bij->tbj/dot_general | solution.py:65
  270.6 18.5 %scatter_fusion.2 = f32[192,32,128]{2,0,1:T(8,128)S(1)} fusion(f32[192,32,128]{2,0,1:T(8,128)S(1)} %broadcast_in_dim.36.clone, s32[112]{0:T(128)S(1)} %get-tuple-element.33, f32[112,192,128]{2,1,0:T(8,128)} %fusion.13), kind=kCustom, calls=%fused_computation.7 | custom fusion | flops 2752512 | bytes 33030592 | tf_op jit(solution)/shard_map/scatter-add | solution.py:66
  290.6 8.7 %convert_bitcast_fusion.5 = bf16[112,1,128,128]{3,2,0,1:T(8,128)(2,1)} fusion(bf16[112,192,128]{2,1,0:T(8,128)(2,1)} %gather_fusion.4, pred[112]{0:T(512)(128)(4,1)S(1)} %get-tuple-element.18, bf16[112,192,128]{2,1,0:T(8,128)(2,1)} %gather_fusion, pred[112]{0:T(512)(128)(4,1)S(1)} %get-tuple-element.30), kind=kOutput, calls=%fused_computation.60 | convolution fusion | flops 711983104 | bytes 14680288 | tf_op jit(solution)/shard_map/tbi,tbj->bij/dot_general | solution.py:102
  299.3 8.8 %convert_bitcast_fusion.6 = bf16[112,1,128,128]{3,2,0,1:T(8,128)(2,1)} fusion(bf16[112,192,128]{2,1,0:T(8,128)(2,1)} %gather_fusion.3, pred[112]{0:T(512)(128)(4,1)S(1)} %get-tuple-element.18, bf16[112,192,128]{2,1,0:T(8,128)(2,1)} %gather_fusion, pred[112]{0:T(512)(128)(4,1)S(1)} %get-tuple-element.30), kind=kOutput, calls=%fused_computation.61 | convolution fusion | flops 711983104 | bytes 14680288 | tf_op jit(solution)/shard_map/tbi,tbj->bij/dot_general | solution.py:99
  308.2 4.5 convert_bitcast_fusion.4
  312.7 9.7 %pad_maximum_fusion = bf16[112,3,128,128]{3,2,0,1:T(8,128)(2,1)} fusion(bf16[112,1,128,128]{3,2,0,1:T(8,128)(2,1)} %convert_bitcast_fusion.4, bf16[112,1,128,128]{3,2,0,1:T(8,128)(2,1)} %convert_bitcast_fusion.5, bf16[112,1,128,128]{3,2,0,1:T(8,128)(2,1)} %convert_bitcast_fusion.6), kind=kLoop, calls=%fused_computation.10 | loop fusion | flops 11010048 | bytes 22020096 | tf_op jit(solution)/shard_map/stack | solution.py:107
  323.7 18.1 %all-reduce.5.cloned.1.call-done = bf16[192,4096]{1,0:T(8,128)(2,1)} async-done(((bf16[192,4096]{1,0:T(8,128)(2,1)}), bf16[192,4096]{1,0:T(8,128)(2,1)}) %all-reduce.5.cloned.1.call-update) | async-done | bytes 1572880 | tf_op jit(solution)/shard_map/psum | solution.py:113
  341.8 2.8 fusion.35
  344.7 5.9 fusion.39
  350.6 2.7 pad_maximum_fusion.1
  353.9 37.3 %all-reduce.1 = (f32[4]{0:T(128)}, f32[512]{0:T(512)}) all-reduce(f32[4]{0:T(128)S(1)} %pad_maximum_fusion.1, f32[512]{0:T(512)S(1)} %dynamic_slice.32), channel_id=1, replica_groups=mesh['dp'=16,'tensor'=8] {'dp'}, use_global_device_ids=true, to_apply=%region_14.17 | all-reduce | flops 516 | bytes 4128 | tf_op jit(solution)/shard_map/psum | solution.py:123
  394.7 246.3 %all-reduce.7.cloned.1.call-done = bf16[112,3,128,128]{3,2,0,1:T(8,128)(2,1)} async-done(((bf16[112,3,128,128]{3,2,0,1:T(8,128)(2,1)}), bf16[112,3,128,128]{3,2,0,1:T(8,128)(2,1)}) %all-reduce.7.cloned.1.call-update) | async-done | bytes 11010064
  (71 shorter events, 20.2 us)
Async XLA Ops:
  7.2 58.5 %all-gather.4.cloned.1.call-start = ((), (), s32[]{:S(2)}) async-start(), calls=%async_computation.1 | async-start | bytes 3899392 | tf_op jit(solution)/shard_map/all_gather | solution.py:51
  7.9 111.2 %all-gather.6.cloned.1.call-start = ((), (), s32[]{:S(2)}) async-start(), calls=%async_computation.2 | async-start | bytes 3899392 | tf_op jit(solution)/shard_map/all_gather | solution.py:52
  8.7 164.0 %all-gather.8.cloned.1.call-start = ((), (), s32[]{:S(2)}) async-start(), calls=%async_computation.3 | async-start | bytes 3899392 | tf_op jit(solution)/shard_map/all_gather | solution.py:53
  9.4 332.4 %all-reduce.5.cloned.1.call-start = ((), (), s32[]{:S(2)}) async-start(), calls=%async_computation.5 | async-start | bytes 3145728 | tf_op jit(solution)/shard_map/psum | solution.py:113
  20.0 8.0 %slice-start = ((s8[6291456]{0:T(1024)(128)(4,1)}), s8[4194304]{0:T(1024)(128)(4,1)S(1)}, s32[]{:S(2)}) async-start(s8[6291456]{0:T(1024)(128)(4,1)} %bitcast.158), calls=%async_computation.7 | async-start | bytes 8388608
  20.0 8.0 %slice-start.1 = ((s8[6291456]{0:T(1024)(128)(4,1)}), s8[2097152]{0:T(1024)(128)(4,1)S(1)}, s32[]{:S(2)}) async-start(s8[6291456]{0:T(1024)(128)(4,1)} %bitcast.158), calls=%async_computation.8 | async-start | bytes 4194304
  27.3 0.7 copy-start.8
  28.0 5.6 copy-start.7
  35.7 3.8 copy-start.4
  147.0 25.6 %copy-start = (f32[192,14,128]{2,0,1:T(8,128)}, f32[192,14,128]{2,0,1:T(8,128)S(1)}, u32[]{:S(2)}) copy-start(f32[192,14,128]{2,0,1:T(8,128)S(1)} %scatter_fusion.1) | copy-start | bytes 4128772
  213.3 10.4 %copy-start.3 = (bf16[112,192,128]{2,1,0:T(8,128)(2,1)S(1)}, bf16[112,192,128]{2,1,0:T(8,128)(2,1)}, u32[]{:S(2)}) copy-start(bf16[112,192,128]{2,1,0:T(8,128)(2,1)} %gather_fusion.3) | copy-start | bytes 16515076
  255.7 1.1 copy-start.1
  255.7 137.3 %reduce-scatter.5.cloned.1.call-start = ((), (), s32[]{:S(2)}) async-start(), calls=%async_computation.4 | async-start | bytes 1769472 | tf_op jit(solution)/shard_map/reduce_scatter | solution.py:67
  290.5 350.4 %all-reduce.7.cloned.1.call-start = ((), (), s32[]{:S(2)}) async-start(), calls=%async_computation.6 | async-start | bytes 22020096
  290.6 17.6 %slice-start.2 = ((s8[5505024]{0:T(1024)(128)(4,1)}), s8[4194304]{0:T(1024)(128)(4,1)S(1)}, s32[]{:S(2)}) async-start(s8[5505024]{0:T(1024)(128)(4,1)} %bitcast.160), calls=%async_computation.9 | async-start | bytes 8388608
  290.6 17.6 %slice-start.4 = ((s8[5505024]{0:T(1024)(128)(4,1)}), s8[4194304]{0:T(1024)(128)(4,1)S(1)}, s32[]{:S(2)}) async-start(s8[5505024]{0:T(1024)(128)(4,1)} %bitcast.162), calls=%async_computation.11 | async-start | bytes 8388608
  299.3 8.8 %slice-start.3 = ((s8[5505024]{0:T(1024)(128)(4,1)}), s8[1310720]{0:T(1024)(128)(4,1)S(1)}, s32[]{:S(2)}) async-start(s8[5505024]{0:T(1024)(128)(4,1)} %bitcast.160), calls=%async_computation.10 | async-start | bytes 2621440
  299.3 8.8 %slice-start.5 = ((s8[5505024]{0:T(1024)(128)(4,1)}), s8[1310720]{0:T(1024)(128)(4,1)S(1)}, s32[]{:S(2)}) async-start(s8[5505024]{0:T(1024)(128)(4,1)} %bitcast.162), calls=%async_computation.12 | async-start | bytes 2621440
  322.4 0.7 copy-start.9
  322.4 19.4 %copy-start.2 = (f32[192,4096]{1,0:T(8,128)S(1)}, f32[192,4096]{1,0:T(8,128)}, u32[]{:S(2)}) copy-start(f32[192,4096]{1,0:T(8,128)} %get-tuple-element.23) | copy-start | bytes 9437188
  341.8 2.9 copy-start.5
  341.8 2.9 copy-start.6
Sparse Core Ops, SparseCore 0:
  10.4 55.1 all-gather.3
  68.1 50.9 all-gather.5
  121.6 50.9 all-gather.7
  255.8 85.9 all-reduce.4
  344.1 44.9 reduce-scatter.4
  391.5 249.4 all-reduce.6
where the time goes:
time: 659 us; the launch traced here: 650 us
  waiting for transfers between devices  339 us (51%)
  other arithmetic  137 us (21%)
  matrix products  83.2 us (13%)
  blocking collectives  37.3 us (6%)
  local copies, waits for them, and re-layouts  30.1 us (5%)
  between operations  23 us (3%)
    unnamed x7, waiting for transfers between devices  248 us
    psum x1, blocking collectives, per_device(): gain_sum, depth_sum = lax.psum((gain_part, jnp.stack(depth_list)), 'dp')  37.3 us
    all_gather x1, waiting for transfers between devices, per_device(): lax.all_gather(down_blocks, 'dp', axis=0, tiled=True)  25.6 us
    all_gather x1, waiting for transfers between devices, per_device(): lax.all_gather(up_blocks, 'dp', axis=0, tiled=True)  25.2 us
    all_gather x1, waiting for transfers between devices, per_device(): lax.all_gather(gate_blocks, 'dp', axis=0, tiled=True)  22 us
    scatter-add x1, other arithmetic, per_device(): gate_pre = zero_cols.at[:, cols_here].add(gate_part)  18.7 us
    scatter-add x1, other arithmetic, per_device(): ffn3 = zero_rows.at[:, rows_here].add(product)  18.5 us
    scatter-add x1, other arithmetic, per_device(): grad_hidden = zero_cols.at[:, cols_here].add(product)  18.4 us
  transfers between devices with their start and end apart: 6, of which 5 were waited for; matrix products, arithmetic and copies ran while one was open for 25% of the time, Pallas kernels for 0%

commit v1 on v0

--- a/solution.py
+++ b/solution.py
@@ -5,6 +5,13 @@
 
 FF = 14336
 EPSILON = 1e-05
+
+
+def all_by_exchange(x, axis, along):
+    size = lax.axis_size(axis)
+    blocks = jnp.stack([x for _ in range(size)])
+    blocks = lax.all_to_all(blocks, axis, split_axis=0, concat_axis=0)
+    return jnp.concatenate(blocks, axis=along)
 
 
 def norm_rows(mixed, gain):
@@ -50,7 +57,7 @@
     gate_all, up_all, down_all = (
         lax.all_gather(gate_blocks, "dp", axis=0, tiled=True),
         lax.all_gather(up_blocks, "dp", axis=0, tiled=True),
-        lax.all_gather(down_blocks, "dp", axis=0, tiled=True),
+        all_by_exchange(down_blocks, "dp", 0),
     )
     pieces = (gate_all, up_all)
     rows_here, cols_here = select()

time: 659 us -> 630 us (0.956)
  waiting for transfers between devices: 339 us -> 299 us
  starting transfers between devices: 0.24 us -> 8.54 us
    all_gather x1 -> x0, waiting for transfers between devices: 25.6 us -> none  [per_device(): lax.all_gather(down_blocks, 'dp', axis=0, tiled=True)]
    all_gather x1, waiting for transfers between devices: 22 us -> 0.02 us  [per_device(): lax.all_gather(gate_blocks, 'dp', axis=0, tiled=True)]
    all_to_all x0 -> x1, waiting for transfers between devices: none -> 16.1 us  [all_by_exchange(): blocks = lax.all_to_all(blocks, axis, split_axis=0, concat_axis=0)]
    all_to_all x0 -> x1, starting transfers between devices: none -> 8.34 us  [all_by_exchange(): blocks = lax.all_to_all(blocks, axis, split_axis=0, concat_axis=0)]
    all_gather x1, waiting for transfers between devices: 25.2 us -> 17.5 us  [per_device(): lax.all_gather(up_blocks, 'dp', axis=0, tiled=True)]
    unnamed x7 -> x6, waiting for transfers between devices: 248 us -> 248 us
  transfers between devices with their start and end apart: 6 -> 6, of which waited for: 5 -> 4; matrix products, arithmetic and copies ran while one was open for 25% -> 27% of each run, Pallas kernels for 0% -> 0%
where the time goes in v1:
time: 630 us; the launch traced here: 621 us
  waiting for transfers between devices  299 us (47%)
  other arithmetic  137 us (22%)
  matrix products  83.9 us (13%)
  blocking collectives  37.2 us (6%)
  local copies, waits for them, and re-layouts  32 us (5%)
  between operations  22.7 us (4%)
  starting transfers between devices  8.54 us (1%)
    unnamed x6, waiting for transfers between devices  248 us
    psum x1, blocking collectives, per_device(): gain_sum, depth_sum = lax.psum((gain_part, jnp.stack(depth_list)), 'dp')  37.2 us
    scatter-add x1, other arithmetic, per_device(): grad_hidden = zero_cols.at[:, cols_here].add(product)  18.9 us
    scatter-add x1, other arithmetic, per_device(): ffn3 = zero_rows.at[:, rows_here].add(product)  18.5 us
    scatter-add x1, other arithmetic, per_device(): up_pre = zero_cols.at[:, cols_here].add(up_part)  18.4 us
    psum x1, waiting for transfers between devices, per_device(): lax.psum(grad_normed.astype(jnp.bfloat16), 'tensor').astype(jnp.float32)  18.3 us
    scatter-add x1, other arithmetic, per_device(): grad_normed3 = zero_rows.at[:, rows_here].add(contrib)  18.3 us
    scatter-add x1, other arithmetic, per_device(): gate_pre = zero_cols.at[:, cols_here].add(gate_part)  18.2 us
  transfers between devices with their start and end apart: 6, of which 4 were waited for; matrix products, arithmetic and copies ran while one was open for 27% of the time, Pallas kernels for 0%

profile of v1, /device:TPU:0, one launch (start us, length us, event | category | flops | bytes accessed | tf_op | source)
XLA Modules:
  0.0 620.9 jit_solution(16953657523187734614)
XLA Ops:
  8.7 3.6 stack.24
  12.3 8.3 %all-to-all-start = ((bf16[16,7,128,128]{3,2,1,0:T(8,128)(2,1)}), bf16[16,7,128,128]{3,2,1,0:T(8,128)(2,1)}, u32[]{:S(2)}, u32[]{:S(2)}) async-start(bf16[16,7,128,128]{3,2,1,0:T(8,128)(2,1)} %stack.24), calls=%async_computation | async-start | bytes 7340032 | tf_op jit(solution)/shard_map/all_to_all | solution.py:13
  29.7 7.2 %fusion.43 = f32[24,8,32,128]{3,1,2,0:T(8,128)S(1)} fusion(f32[]{:T(128)} %bitcast.9, f32[]{:T(128)} %bitcast.6, f32[]{:T(128)} %bitcast.3, f32[]{:T(128)} %bitcast, bf16[4,192,4096]{2,1,0:T(8,128)(2,1)} %param.13, s32[]{:T(128)S(6)} %select_n.49, s32[]{:T(128)S(6)} %select_n.48, s32[]{:T(128)S(6)} %select_n.47, s32[]{:T(128)S(6)} %select_n.46), kind=kLoop, calls=%fused_computation.71 | loop fusion | flops 8650752 | bytes 9437216
  37.6 5.6 multiply_reduce_fusion
  45.3 3.7 gather_fusion
  49.4 3.7 gather_fusion.2
  53.2 16.1 %all-to-all-done = bf16[16,7,128,128]{3,2,1,0:T(8,128)(2,1)} async-done(((bf16[16,7,128,128]{3,2,1,0:T(8,128)(2,1)}), bf16[16,7,128,128]{3,2,1,0:T(8,128)(2,1)}, u32[]{:S(2)}, u32[]{:S(2)}) %all-to-all-start) | async-done | bytes 3670048 | tf_op jit(solution)/shard_map/all_to_all | solution.py:13
  69.2 10.4 %fusion.10 = f32[112,192,128]{2,1,0:T(8,128)} fusion(bf16[112,128,128]{2,1,0:T(8,128)(2,1)} %bitcast.19, bf16[112,192,128]{2,1,0:T(8,128)(2,1)} %gather_fusion.2, pred[112]{0:T(512)(128)(4,1)S(1)} %get-tuple-element.30), kind=kOutput, calls=%fused_computation.21 | convolution fusion | flops 707395584 | bytes 20185200 | tf_op jit(solution)/shard_map/tbj,bij->tbi/dot_general | solution.py:84
  79.7 18.9 %scatter_fusion.3 = f32[192,14,128]{2,0,1:T(8,128)S(1)} fusion(f32[192,14,128]{2,0,1:T(8,128)S(1)} %broadcast_in_dim.37.clone.1, s32[112]{0:T(128)S(1)} %get-tuple-element.32, f32[112,192,128]{2,1,0:T(8,128)} %fusion.10), kind=kCustom, calls=%fused_computation.8 | custom fusion | flops 2752512 | bytes 33030592 | tf_op jit(solution)/shard_map/scatter-add | solution.py:85
  98.7 9.7 %fusion.19 = f32[112,192,128]{2,1,0:T(8,128)} fusion(bf16[112,128,128]{2,1,0:T(8,128)(2,1)} %all-gather.3.cloned.1.call-done, bf16[112,192,128]{2,1,0:T(8,128)(2,1)} %gather_fusion, pred[112]{0:T(512)(128)(4,1)S(1)} %get-tuple-element.30), kind=kOutput, calls=%fused_computation.30 | convolution fusion | flops 707395584 | bytes 20185200 | tf_op jit(solution)/shard_map/tbi,bij->tbj/dot_general | solution.py:65
  108.5 18.2 %scatter_fusion = f32[192,14,128]{2,0,1:T(8,128)S(1)} fusion(f32[192,14,128]{2,0,1:T(8,128)S(1)} %broadcast_in_dim.37.clone, s32[112]{0:T(128)S(1)} %get-tuple-element.32, f32[112,192,128]{2,1,0:T(8,128)} %fusion.19), kind=kCustom, calls=%fused_computation.5 | custom fusion | flops 2752512 | bytes 33030592 | tf_op jit(solution)/shard_map/scatter-add | solution.py:67
  126.7 17.5 %all-gather.5.cloned.1.call-done = bf16[112,128,128]{2,1,0:T(8,128)(2,1)} async-done(((bf16[7,128,128]{2,1,0:T(8,128)(2,1)}), bf16[112,128,128]{2,1,0:T(8,128)(2,1)}) %all-gather.5.cloned.1.call-update) | async-done | bytes 3670032 | tf_op jit(solution)/shard_map/all_gather | solution.py:59
  144.2 9.5 %fusion.17 = f32[112,192,128]{2,1,0:T(8,128)} fusion(bf16[112,128,128]{2,1,0:T(8,128)(2,1)} %all-gather.5.cloned.1.call-done, bf16[112,192,128]{2,1,0:T(8,128)(2,1)} %gather_fusion, pred[112]{0:T(512)(128)(4,1)S(1)} %get-tuple-element.30), kind=kOutput, calls=%fused_computation.28 | convolution fusion | flops 707395584 | bytes 20185200 | tf_op jit(solution)/shard_map/tbi,bij->tbj/dot_general | solution.py:66
  153.8 18.4 %scatter_fusion.1 = f32[192,14,128]{2,0,1:T(8,128)S(1)} fusion(f32[192,14,128]{2,0,1:T(8,128)S(1)} %broadcast_in_dim.37.clone.2, s32[112]{0:T(128)S(1)} %get-tuple-element.32, f32[112,192,128]{2,1,0:T(8,128)} %fusion.17), kind=kCustom, calls=%fused_computation.6 | custom fusion | flops 2752512 | bytes 33030592 | tf_op jit(solution)/shard_map/scatter-add | solution.py:68
  172.2 3.4 multiply_convert_fusion.1
  175.5 4.8 gather_fusion.4
  180.3 3.8 gather_fusion.3
  184.1 10.5 %fusion.2 = f32[112,192,128]{2,1,0:T(8,128)} fusion(bf16[112,128,128]{2,1,0:T(8,128)(2,1)} %all-gather.5.cloned.1.call-done, bf16[112,192,128]{2,1,0:T(8,128)(2,1)} %gather_fusion.4, pred[112]{0:T(512)(128)(4,1)S(1)} %get-tuple-element.18), kind=kOutput, calls=%fused_computation.13 | convolution fusion | flops 707395584 | bytes 20185200 | tf_op jit(solution)/shard_map/tbj,bij->tbi/dot_general | solution.py:96
  194.6 12.1 %fusion.29 = f32[112,192,128]{2,1,0:T(8,128)} fusion(f32[112,192,128]{2,1,0:T(8,128)} %fusion.2, bf16[112,128,128]{2,1,0:T(8,128)(2,1)} %all-gather.3.cloned.1.call-done, bf16[112,192,128]{2,1,0:T(8,128)(2,1)S(1)} %copy-done.3, pred[112]{0:T(512)(128)(4,1)S(1)} %get-tuple-element.18), kind=kOutput, calls=%fused_computation.56 | convolution fusion | flops 710148096 | bytes 31195248 | tf_op jit(solution)/shard_map/tbj,bij->tbi/dot_general | solution.py:95
  207.0 18.3 %scatter_fusion.4 = f32[192,32,128]{2,0,1:T(8,128)S(1)} fusion(f32[192,32,128]{2,0,1:T(8,128)S(1)} %broadcast_in_dim.36.clone.1, s32[112]{0:T(128)S(1)} %get-tuple-element.33, f32[112,192,128]{2,1,0:T(8,128)} %fusion.29), kind=kCustom, calls=%fused_computation.9 | custom fusion | flops 2752512 | bytes 33030592 | tf_op jit(solution)/shard_map/scatter-add | solution.py:99
  227.7 3.8 gather_fusion.1
  231.5 9.7 %fusion.13 = f32[112,192,128]{2,1,0:T(8,128)} fusion(bf16[112,128,128]{2,1,0:T(8,128)(2,1)} %bitcast.19, bf16[112,192,128]{2,1,0:T(8,128)(2,1)} %gather_fusion.1, pred[112]{0:T(512)(128)(4,1)S(1)} %get-tuple-element.18), kind=kOutput, calls=%fused_computation.24 | convolution fusion | flops 707395584 | bytes 20185200 | tf_op jit(solution)/shard_map/tbi,bij->tbj/dot_general | solution.py:72
  241.5 18.5 %scatter_fusion.2 = f32[192,32,128]{2,0,1:T(8,128)S(1)} fusion(f32[192,32,128]{2,0,1:T(8,128)S(1)} %broadcast_in_dim.36.clone, s32[112]{0:T(128)S(1)} %get-tuple-element.33, f32[112,192,128]{2,1,0:T(8,128)} %fusion.13), kind=kCustom, calls=%fused_computation.7 | custom fusion | flops 2752512 | bytes 33030592 | tf_op jit(solution)/shard_map/scatter-add | solution.py:73
  261.6 8.8 %convert_bitcast_fusion.5 = bf16[112,1,128,128]{3,2,0,1:T(8,128)(2,1)} fusion(bf16[112,192,128]{2,1,0:T(8,128)(2,1)} %gather_fusion.4, pred[112]{0:T(512)(128)(4,1)S(1)} %get-tuple-element.18, bf16[112,192,128]{2,1,0:T(8,128)(2,1)} %gather_fusion, pred[112]{0:T(512)(128)(4,1)S(1)} %get-tuple-element.30), kind=kOutput, calls=%fused_computation.60 | convolution fusion | flops 711983104 | bytes 14680288 | tf_op jit(solution)/shard_map/tbi,tbj->bij/dot_general | solution.py:109
  270.3 8.8 %convert_bitcast_fusion.6 = bf16[112,1,128,128]{3,2,0,1:T(8,128)(2,1)} fusion(bf16[112,192,128]{2,1,0:T(8,128)(2,1)} %gather_fusion.3, pred[112]{0:T(512)(128)(4,1)S(1)} %get-tuple-element.18, bf16[112,192,128]{2,1,0:T(8,128)(2,1)} %gather_fusion, pred[112]{0:T(512)(128)(4,1)S(1)} %get-tuple-element.30), kind=kOutput, calls=%fused_computation.61 | convolution fusion | flops 711983104 | bytes 14680288 | tf_op jit(solution)/shard_map/tbi,tbj->bij/dot_general | solution.py:106
  279.2 4.5 convert_bitcast_fusion.4
  283.7 9.7 %pad_maximum_fusion = bf16[112,3,128,128]{3,2,0,1:T(8,128)(2,1)} fusion(bf16[112,1,128,128]{3,2,0,1:T(8,128)(2,1)} %convert_bitcast_fusion.4, bf16[112,1,128,128]{3,2,0,1:T(8,128)(2,1)} %convert_bitcast_fusion.5, bf16[112,1,128,128]{3,2,0,1:T(8,128)(2,1)} %convert_bitcast_fusion.6), kind=kLoop, calls=%fused_computation.10 | loop fusion | flops 11010048 | bytes 22020096 | tf_op jit(solution)/shard_map/stack | solution.py:114
  294.7 18.3 %all-reduce.5.cloned.1.call-done = bf16[192,4096]{1,0:T(8,128)(2,1)} async-done(((bf16[192,4096]{1,0:T(8,128)(2,1)}), bf16[192,4096]{1,0:T(8,128)(2,1)}) %all-reduce.5.cloned.1.call-update) | async-done | bytes 1572880 | tf_op jit(solution)/shard_map/psum | solution.py:120
  313.0 2.8 fusion.35
  315.9 5.9 fusion.39
  325.1 37.2 %all-reduce.1 = (f32[4]{0:T(128)}, f32[512]{0:T(512)}) all-reduce(f32[4]{0:T(128)S(1)} %pad_maximum_fusion.1, f32[512]{0:T(512)S(1)} %dynamic_slice.32), channel_id=1, replica_groups=mesh['dp'=16,'tensor'=8] {'dp'}, use_global_device_ids=true, to_apply=%region_14.17 | all-reduce | flops 516 | bytes 4128 | tf_op jit(solution)/shard_map/psum | solution.py:130
  365.7 246.1 %all-reduce.7.cloned.1.call-done = bf16[112,3,128,128]{3,2,0,1:T(8,128)(2,1)} async-done(((bf16[112,3,128,128]{3,2,0,1:T(8,128)(2,1)}), bf16[112,3,128,128]{3,2,0,1:T(8,128)(2,1)}) %all-reduce.7.cloned.1.call-update) | async-done | bytes 11010064
  (75 shorter events, 20.6 us)
Async XLA Ops:
  7.2 91.5 %all-gather.3.cloned.1.call-start = ((), (), s32[]{:S(2)}) async-start(), calls=%async_computation.2 | async-start | bytes 3899392 | tf_op jit(solution)/shard_map/all_gather | solution.py:58
  7.9 136.2 %all-gather.5.cloned.1.call-start = ((), (), s32[]{:S(2)}) async-start(), calls=%async_computation.3 | async-start | bytes 3899392 | tf_op jit(solution)/shard_map/all_gather | solution.py:59
  12.3 8.4 %copy-start.8 = (s32[4]{0:T(128)S(1)}, s32[4]{0:T(128)}, u32[]{:S(2)}) copy-start(s32[4]{0:T(128)} %param.15) | copy-start | bytes 52
  12.3 16.8 %copy-start.9 = (f32[4]{0:T(128)S(1)}, f32[4]{0:T(128)}, u32[]{:S(2)}) copy-start(f32[4]{0:T(128)} %param.14) | copy-start | bytes 52
  12.3 56.9 %all-to-all-start = ((bf16[16,7,128,128]{3,2,1,0:T(8,128)(2,1)}), bf16[16,7,128,128]{3,2,1,0:T(8,128)(2,1)}, u32[]{:S(2)}, u32[]{:S(2)}) async-start(bf16[16,7,128,128]{3,2,1,0:T(8,128)(2,1)} %stack.24), calls=%async_computation | async-start | bytes 7340032 | tf_op jit(solution)/shard_map/all_to_all | solution.py:13
  20.6 292.3 %all-reduce.5.cloned.1.call-start = ((), (), s32[]{:S(2)}) async-start(), calls=%async_computation.5 | async-start | bytes 3145728 | tf_op jit(solution)/shard_map/psum | solution.py:120
  29.7 7.9 %slice-start = ((s8[6291456]{0:T(1024)(128)(4,1)}), s8[4194304]{0:T(1024)(128)(4,1)S(1)}, s32[]{:S(2)}) async-start(s8[6291456]{0:T(1024)(128)(4,1)} %bitcast.159), calls=%async_computation.7 | async-start | bytes 8388608
  29.7 7.9 %slice-start.1 = ((s8[6291456]{0:T(1024)(128)(4,1)}), s8[2097152]{0:T(1024)(128)(4,1)S(1)}, s32[]{:S(2)}) async-start(s8[6291456]{0:T(1024)(128)(4,1)} %bitcast.159), calls=%async_computation.8 | async-start | bytes 4194304
  36.9 0.7 copy-start.10
  37.6 5.6 copy-start.7
  45.3 3.7 copy-start.4
  126.7 17.5 %copy-start = (f32[192,14,128]{2,0,1:T(8,128)}, f32[192,14,128]{2,0,1:T(8,128)S(1)}, u32[]{:S(2)}) copy-start(f32[192,14,128]{2,0,1:T(8,128)S(1)} %scatter_fusion) | copy-start | bytes 4128772
  184.1 10.5 %copy-start.3 = (bf16[112,192,128]{2,1,0:T(8,128)(2,1)S(1)}, bf16[112,192,128]{2,1,0:T(8,128)(2,1)}, u32[]{:S(2)}) copy-start(bf16[112,192,128]{2,1,0:T(8,128)(2,1)} %gather_fusion.3) | copy-start | bytes 16515076
  226.6 1.1 copy-start.1
  226.6 137.5 %reduce-scatter.5.cloned.1.call-start = ((), (), s32[]{:S(2)}) async-start(), calls=%async_computation.4 | async-start | bytes 1769472 | tf_op jit(solution)/shard_map/reduce_scatter | solution.py:74
  261.5 350.3 %all-reduce.7.cloned.1.call-start = ((), (), s32[]{:S(2)}) async-start(), calls=%async_computation.6 | async-start | bytes 22020096
  261.5 17.6 %slice-start.2 = ((s8[5505024]{0:T(1024)(128)(4,1)}), s8[4194304]{0:T(1024)(128)(4,1)S(1)}, s32[]{:S(2)}) async-start(s8[5505024]{0:T(1024)(128)(4,1)} %bitcast.161), calls=%async_computation.9 | async-start | bytes 8388608
  261.5 17.6 %slice-start.4 = ((s8[5505024]{0:T(1024)(128)(4,1)}), s8[4194304]{0:T(1024)(128)(4,1)S(1)}, s32[]{:S(2)}) async-start(s8[5505024]{0:T(1024)(128)(4,1)} %bitcast.163), calls=%async_computation.11 | async-start | bytes 8388608
  270.3 8.8 %slice-start.3 = ((s8[5505024]{0:T(1024)(128)(4,1)}), s8[1310720]{0:T(1024)(128)(4,1)S(1)}, s32[]{:S(2)}) async-start(s8[5505024]{0:T(1024)(128)(4,1)} %bitcast.161), calls=%async_computation.10 | async-start | bytes 2621440
  270.3 8.8 %slice-start.5 = ((s8[5505024]{0:T(1024)(128)(4,1)}), s8[1310720]{0:T(1024)(128)(4,1)S(1)}, s32[]{:S(2)}) async-start(s8[5505024]{0:T(1024)(128)(4,1)} %bitcast.163), calls=%async_computation.12 | async-start | bytes 2621440
  293.4 0.7 copy-start.11
  293.4 19.6 %copy-start.2 = (f32[192,4096]{1,0:T(8,128)S(1)}, f32[192,4096]{1,0:T(8,128)}, u32[]{:S(2)}) copy-start(f32[192,4096]{1,0:T(8,128)} %get-tuple-element.23) | copy-start | bytes 9437188
  313.0 2.9 copy-start.5
  313.0 2.9 copy-start.6
Sparse Core Ops, SparseCore 0:
  10.4 80.1 all-gather.2
  93.1 50.9 all-gather.4
  226.7 86.1 all-reduce.4
  315.2 45.4 reduce-scatter.4
  363.1 248.6 all-reduce.6
